TPU v7x, 256 devices: a whole 4x4x8 slice. The times are simulated.
256 devices in a mesh: leaf: 64 (over x, z, core), front: 4 (over y).
Axes of the slice: x: 4, y: 4, z: 8, core: 2. Of those that a mesh axis runs over, the one named last changes fastest.
Arguments:
- leaf_update: float32 [65536, 1024], P('leaf'), as said below
- separator_rows_1: float32 [16384, 1536], P(('leaf', 'front')), as said below
- remaining_rows_1: float32 [32768, 1536], P(('leaf', 'front'))
- separator_rows_2: float32 [8192, 1536], P(('leaf', 'front')), as said below
- remaining_rows_2: float32 [16384, 1536], P(('leaf', 'front'))
- separator_rows_3: float32 [4096, 1536], P(('leaf', 'front')), as said below
- remaining_rows_3: float32 [8192, 1536], P(('leaf', 'front'))
- child_map_1: int32 [64, 8], replicated, may hold values from 0 to 11, as said below
- child_map_2: int32 [32, 8], replicated, may hold values from 0 to 11, as said below
- child_map_3: int32 [16, 8], replicated, may hold values from 0 to 11, as said below
Outputs:
- pivot_factor_1: float32 [16384, 512], P(('leaf', 'front'))
- below_factor_1: float32 [32768, 512], P(('leaf', 'front'))
- pivot_factor_2: float32 [8192, 512], P(('leaf', 'front'))
- below_factor_2: float32 [16384, 512], P(('leaf', 'front'))
- pivot_factor_3: float32 [4096, 512], P(('leaf', 'front'))
- below_factor_3: float32 [8192, 512], P(('leaf', 'front'))
Inputs may be any that keep to these rules, and one draw needn't show every extreme that they name: `child_map_1`: each row lists 8 distinct parent tiles in increasing order, the last one always 12 - 1. `child_map_2`: each row lists 8 distinct parent tiles in increasing order, the last one always 12 - 1. `child_map_3`: each row lists 8 distinct parent tiles in increasing order, the last one always 12 - 1. `leaf_update`: each block is symmetric positive definite, diagonal between 0.5 and 2, off-diagonal entries of magnitude about 0.008, smallest eigenvalue about 0.1 or more. Each front, separator_rows_1 above remaining_rows_1, is symmetric positive definite, diagonal between 2 and 4, off-diagonal entries of magnitude about 0.03, smallest eigenvalue about 0.35 or more. Each front, separator_rows_2 above remaining_rows_2, is symmetric positive definite, diagonal between 2 and 4, off-diagonal entries of magnitude about 0.03, smallest eigenvalue about 0.35 or more. Each front, separator_rows_3 above remaining_rows_3, is symmetric positive definite, diagonal between 2 and 4, off-diagonal entries of magnitude about 0.03, smallest eigenvalue about 0.35 or more.
All inputs are finite; a program needn't handle non-finite values.
Results may differ from a plain program's by a relative error of at most 0.0003.
Values sent between devices are 32-bit elements; how exact they have to be, the bound alone decides.
No kernel may reach another device: no remote copies, remote signals or barrier semaphores. Data moves between devices by JAX's collectives and lax.ppermute only.
A program may use at most 128 MiB of HBM per device.

v0:
```python
import jax
import jax.numpy as jnp
from jax import lax
from jax.sharding import PartitionSpec as P

TILE = 128
SEP = 512
UPD = 1024
NF = 1536
NT = 12
UT = 8


def from_partner(block, axis, stride):
    count = lax.axis_size(axis)
    route = []
    for low in range(count):
        high = low | 1 << stride
        if high != low and high < count:
            route += [(low, high), (high, low)]
    return lax.ppermute(block, axis, route)


def collect(pieces, depth_count):
    gathered = lax.all_gather(pieces, "front", axis=0, tiled=True)
    leaf_place = lax.axis_index("leaf")
    for bit_number in range(depth_count):
        partner = from_partner(gathered, "leaf", bit_number)
        on_high = leaf_place >> bit_number & 1 == 1
        gathered = jnp.where(
            on_high,
            jnp.concatenate([partner, gathered], axis=0),
            jnp.concatenate([gathered, partner], axis=0),
        )
    return gathered


def owned_rows(position, group_count):
    sep_count = SEP // group_count
    upd_count = UPD // group_count
    sep_index = position * sep_count + jnp.arange(sep_count, dtype=jnp.int32)
    upd_index = SEP + position * upd_count + jnp.arange(upd_count, dtype=jnp.int32)
    return jnp.concatenate([sep_index, upd_index])


def locate(tile_map, targets):
    tile_of = targets // TILE
    offset = targets % TILE
    matches = tile_map[None, :] == tile_of[:, None]
    present = jnp.any(matches, axis=1)
    slot_ids = jnp.arange(tile_map.shape[0], dtype=jnp.int32)
    source = jnp.sum(jnp.where(matches, slot_ids[None, :], 0), axis=1)
    return (source * TILE + offset, present)


def select_rows(full_update, tile_map, targets):
    source, present = locate(tile_map, targets)
    return jnp.where(present[:, None], jnp.take(full_update, source, axis=0), 0.0)


def expand_columns(row_block, tile_map):
    placing = (tile_map[:, None] == jnp.arange(NT, dtype=jnp.int32)[None, :]).astype(jnp.float32)
    tiled = row_block.reshape(row_block.shape[0], UT, TILE)
    placed = jnp.einsum("rut,un->rnt", tiled, placing, precision=lax.Precision.HIGHEST)
    return placed.reshape(row_block.shape[0], NF)


def body(
    leaf_update,
    separator_rows_1,
    remaining_rows_1,
    separator_rows_2,
    remaining_rows_2,
    separator_rows_3,
    remaining_rows_3,
    child_map_1,
    child_map_2,
    child_map_3,
):
    leaf_place = lax.axis_index("leaf")
    front_place = lax.axis_index("front")
    front_count = lax.axis_size("front")
    child_full = leaf_update
    sections = (
        (separator_rows_1, remaining_rows_1, child_map_1),
        (separator_rows_2, remaining_rows_2, child_map_2),
        (separator_rows_3, remaining_rows_3, child_map_3),
    )
    results = []
    for level_number in range(1, 4):
        sep_part, upd_part, child_maps = sections[level_number - 1]
        group_count = front_count * 2**level_number
        sep_count = SEP // group_count
        upd_count = UPD // group_count
        pair_bit = level_number - 1
        child_front = leaf_place >> pair_bit
        sibling_front = child_front ^ 1
        position = leaf_place % 2**level_number * front_count + front_place
        own_map = lax.dynamic_index_in_dim(child_maps, child_front, 0, keepdims=False)
        targets = owned_rows(position, group_count)
        sibling_map = lax.dynamic_index_in_dim(child_maps, sibling_front, 0, keepdims=False)
        sibling_full = from_partner(child_full, "leaf", pair_bit)
        sibling_block = select_rows(sibling_full, sibling_map, targets)
        own_term = expand_columns(select_rows(child_full, own_map, targets), own_map)
        sibling_term = expand_columns(sibling_block, sibling_map)
        is_odd = child_front & 1 == 1
        earlier_term = jnp.where(is_odd, sibling_term, own_term)
        later_term = jnp.where(is_odd, own_term, sibling_term)
        front_rows = jnp.concatenate([sep_part, upd_part], axis=0) + earlier_term + later_term
        panel_all = collect(front_rows[:, :SEP], level_number)
        blocks = panel_all.reshape(group_count, sep_count + upd_count, SEP)
        pivot_block = blocks[:, :sep_count].reshape(SEP, SEP)
        lower_block = blocks[:, sep_count:].reshape(UPD, SEP)
        diag_factor = jnp.linalg.cholesky(pivot_block)
        solved_all = lax.linalg.triangular_solve(
            diag_factor, lower_block, left_side=False, lower=True, transpose_a=True
        )
        solved_own = lax.dynamic_slice_in_dim(solved_all, position * upd_count, upd_count, 0)
        results.append(lax.dynamic_slice_in_dim(diag_factor, position * sep_count, sep_count, 0))
        results.append(solved_own)
        if level_number < 3:
            update_own = front_rows[sep_count:, SEP:] - jnp.dot(
                solved_own, solved_all.T, precision=lax.Precision.HIGHEST
            )
            child_full = collect(update_own, level_number)
    return (results[0], results[1], results[2], results[3], results[4], results[5])


def solution(mesh):
    in_specs = (
        P("leaf", None),
        P(("leaf", "front"), None),
        P(("leaf", "front"), None),
        P(("leaf", "front"), None),
        P(("leaf", "front"), None),
        P(("leaf", "front"), None),
        P(("leaf", "front"), None),
        P(),
        P(),
        P(),
    )
    out_specs = (
        P(("leaf", "front"), None),
        P(("leaf", "front"), None),
        P(("leaf", "front"), None),
        P(("leaf", "front"), None),
        P(("leaf", "front"), None),
        P(("leaf", "front"), None),
    )
    return jax.shard_map(body, mesh=mesh, in_specs=in_specs, out_specs=out_specs, check_vma=False)
```

profile of v0, /device:TPU:1, one launch (start us, length us, event | category | flops | bytes accessed | tf_op | source)
XLA Modules:
  0.0 1112.1 jit_solution(10254888534688105837)
XLA Ops:
  25.7 30.1 %all-gather.4.cloned.1.call-done = f32[768,512]{1,0:T(8,128)} async-done(((f32[192,512]{1,0:T(8,128)}), f32[768,512]{1,0:T(8,128)}) %all-gather.4.cloned.1.call-update) | async-done | bytes 1572880 | tf_op jit(solution)/shard_map/all_gather | solution.py:25
  66.7 11.7 %cholesky.374 = f32[128,128]{1,0:T(8,128)S(1)} custom-call(f32[128,128]{1,0:T(8,128)S(1)} %cholesky.586), custom_call_target="Cholesky" | custom-call | tf_op jit(solution)/shard_map/jit(cholesky)/cholesky | solution.py:114
  90.9 11.7 %cholesky.393 = f32[128,128]{1,0:T(8,128)S(1)} custom-call(f32[128,128]{1,0:T(8,128)S(1)} %cholesky.590), custom_call_target="Cholesky" | custom-call | tf_op jit(solution)/shard_map/jit(cholesky)/cholesky | solution.py:114
  102.7 10.0 custom-call.32
  114.2 11.7 %cholesky.414 = f32[128,128]{1,0:T(8,128)S(1)} custom-call(f32[128,128]{1,0:T(8,128)S(1)} %cholesky.595), custom_call_target="Cholesky" | custom-call | tf_op jit(solution)/shard_map/jit(cholesky)/cholesky | solution.py:114
  137.2 12.1 %cholesky.431 = f32[128,128]{1,0:T(8,128)S(1)} custom-call(f32[128,128]{1,0:T(8,128)S(1)} %convolution_subtract_fusion.10), custom_call_target="Cholesky" | custom-call | tf_op jit(solution)/shard_map/jit(cholesky)/cholesky | solution.py:114
  156.1 11.6 %while.6 = (s32[]{:T(128)}, f32[512,512]{1,0:T(8,128)}, s32[4,2]{0,1:T(2,128)S(1)}, f32[4,128,128]{2,1,0:T(8,128)S(1)}, s32[]{:T(128)}) while((s32[]{:T(128)}, f32[512,512]{1,0:T(8,128)}, s32[4,2]{0,1:T(2,128)S(1)}, f32[4,128,128]{2,1,0:T(8,128)S(1)}, s32[]{:T(128)}) %tuple.112), condition=%wide.while_cond, body=%wide.while_body.sunk | while | flops 2 | bytes 131189 | solution.py:115
  167.7 39.3 %custom-call.34 = f32[4,128,128]{1,2,0:T(8,128)S(1)} custom-call(f32[4,128,128]{2,1,0:T(8,128)S(1)} %get-tuple-element.31), custom_call_target="InvertDiagBlocksLowerTriangular" | custom-call | tf_op jit(solution)/shard_map/triangular_solve/custom-call.3 | solution.py:115
  222.2 33.3 %all-gather.6.cloned.1.call-done = f32[512,1024]{1,0:T(8,128)} async-done(((f32[128,1024]{1,0:T(8,128)}), f32[512,1024]{1,0:T(8,128)}) %all-gather.6.cloned.1.call-update) | async-done | bytes 2097168 | tf_op jit(solution)/shard_map/all_gather | solution.py:25
  270.9 86.6 %collective-permute-done.3 = f32[1024,1024]{1,0:T(8,128)} collective-permute-done((f32[1024,1024]{1,0:T(8,128)}, f32[1024,1024]{1,0:T(8,128)}, u32[]{:S(2)}, u32[]{:S(2)}) %collective-permute-start.3) | collective-permute-done | bytes 4194336 | tf_op jit(solution)/shard_map/ppermute | solution.py:21
  362.2 10.7 all_gather.17
  381.1 34.3 %collective-permute-done.5 = f32[768,512]{1,0:T(8,128)S(1)} collective-permute-done((f32[768,512]{1,0:T(8,128)S(1)}, f32[768,512]{1,0:T(8,128)S(1)}, u32[]{:S(2)}, u32[]{:S(2)}) %collective-permute-start.5) | collective-permute-done | bytes 1572896 | tf_op jit(solution)/shard_map/ppermute | solution.py:21
  419.8 11.7 %cholesky.446 = f32[128,128]{1,0:T(8,128)S(1)} custom-call(f32[128,128]{1,0:T(8,128)S(1)} %cholesky.599), custom_call_target="Cholesky" | custom-call | tf_op jit(solution)/shard_map/jit(cholesky)/cholesky | solution.py:114
  444.0 11.7 %cholesky.465 = f32[128,128]{1,0:T(8,128)S(1)} custom-call(f32[128,128]{1,0:T(8,128)S(1)} %cholesky.603), custom_call_target="Cholesky" | custom-call | tf_op jit(solution)/shard_map/jit(cholesky)/cholesky | solution.py:114
  455.7 10.2 custom-call.36
  467.5 11.7 %cholesky.486 = f32[128,128]{1,0:T(8,128)S(1)} custom-call(f32[128,128]{1,0:T(8,128)S(1)} %cholesky.608), custom_call_target="Cholesky" | custom-call | tf_op jit(solution)/shard_map/jit(cholesky)/cholesky | solution.py:114
  490.5 11.9 %cholesky.503 = f32[128,128]{1,0:T(8,128)S(1)} custom-call(f32[128,128]{1,0:T(8,128)S(1)} %convolution_subtract_fusion.9), custom_call_target="Cholesky" | custom-call | tf_op jit(solution)/shard_map/jit(cholesky)/cholesky | solution.py:114
  509.1 11.6 %while.7 = (s32[]{:T(128)}, f32[512,512]{1,0:T(8,128)}, s32[4,2]{0,1:T(2,128)S(1)}, f32[4,128,128]{2,1,0:T(8,128)S(1)}, s32[]{:T(128)}) while((s32[]{:T(128)}, f32[512,512]{1,0:T(8,128)}, s32[4,2]{0,1:T(2,128)S(1)}, f32[4,128,128]{2,1,0:T(8,128)S(1)}, s32[]{:T(128)}) %tuple.127), condition=%wide.while_cond.clone, body=%wide.while_body.clone.sunk | while | flops 2 | bytes 131189 | solution.py:115
  520.7 39.3 %custom-call.38 = f32[4,128,128]{1,2,0:T(8,128)S(1)} custom-call(f32[4,128,128]{2,1,0:T(8,128)S(1)} %get-tuple-element.32), custom_call_target="InvertDiagBlocksLowerTriangular" | custom-call | tf_op jit(solution)/shard_map/triangular_solve/custom-call.3 | solution.py:115
  574.4 26.1 %all-gather.8.cloned.1.call-done = f32[256,1024]{1,0:T(8,128)} async-done(((f32[64,1024]{1,0:T(8,128)}), f32[256,1024]{1,0:T(8,128)}) %all-gather.8.cloned.1.call-update) | async-done | bytes 1048592 | tf_op jit(solution)/shard_map/all_gather | solution.py:25
  608.2 45.6 %collective-permute-done.7 = f32[512,1024]{1,0:T(8,128)S(1)} collective-permute-done((f32[512,1024]{1,0:T(8,128)S(1)}, f32[512,1024]{1,0:T(8,128)S(1)}, u32[]{:S(2)}, u32[]{:S(2)}) %collective-permute-start.7) | collective-permute-done | bytes 2097184 | tf_op jit(solution)/shard_map/ppermute | solution.py:21
  662.4 176.2 %collective-permute-done.8 = f32[1024,1024]{1,0:T(8,128)} collective-permute-done((f32[1024,1024]{1,0:T(8,128)}, f32[1024,1024]{1,0:T(8,128)}, u32[]{:S(2)}, u32[]{:S(2)}) %collective-permute-start.8) | collective-permute-done | bytes 4194336 | tf_op jit(solution)/shard_map/ppermute | solution.py:21
  842.6 10.9 all_gather.19
  858.5 18.7 %collective-permute-done.10 = f32[384,512]{1,0:T(8,128)S(1)} collective-permute-done((f32[384,512]{1,0:T(8,128)S(1)}, f32[384,512]{1,0:T(8,128)S(1)}, u32[]{:S(2)}, u32[]{:S(2)}) %collective-permute-start.10) | collective-permute-done | bytes 786464 | tf_op jit(solution)/shard_map/ppermute | solution.py:21
  885.1 62.8 %collective-permute-done.11 = f32[768,512]{1,0:T(8,128)S(1)} collective-permute-done((f32[768,512]{1,0:T(8,128)S(1)}, f32[768,512]{1,0:T(8,128)S(1)}, u32[]{:S(2)}, u32[]{:S(2)}) %collective-permute-start.11) | collective-permute-done | bytes 1572896 | tf_op jit(solution)/shard_map/ppermute | solution.py:21
  952.3 11.7 %cholesky.518 = f32[128,128]{1,0:T(8,128)S(1)} custom-call(f32[128,128]{1,0:T(8,128)S(1)} %cholesky.612), custom_call_target="Cholesky" | custom-call | tf_op jit(solution)/shard_map/jit(cholesky)/cholesky | solution.py:114
  976.5 11.7 %cholesky.537 = f32[128,128]{1,0:T(8,128)S(1)} custom-call(f32[128,128]{1,0:T(8,128)S(1)} %cholesky.616), custom_call_target="Cholesky" | custom-call | tf_op jit(solution)/shard_map/jit(cholesky)/cholesky | solution.py:114
  988.2 9.9 custom-call.40
  999.8 11.7 %cholesky.558 = f32[128,128]{1,0:T(8,128)S(1)} custom-call(f32[128,128]{1,0:T(8,128)S(1)} %cholesky.621), custom_call_target="Cholesky" | custom-call | tf_op jit(solution)/shard_map/jit(cholesky)/cholesky | solution.py:114
  1022.8 11.9 %cholesky.575 = f32[128,128]{1,0:T(8,128)S(1)} custom-call(f32[128,128]{1,0:T(8,128)S(1)} %convolution_subtract_fusion.8), custom_call_target="Cholesky" | custom-call | tf_op jit(solution)/shard_map/jit(cholesky)/cholesky | solution.py:114
  1041.6 11.5 %while.8 = (s32[]{:T(128)}, f32[512,512]{1,0:T(8,128)}, s32[4,2]{0,1:T(2,128)S(1)}, f32[4,128,128]{2,1,0:T(8,128)S(1)}, s32[]{:T(128)}) while((s32[]{:T(128)}, f32[512,512]{1,0:T(8,128)}, s32[4,2]{0,1:T(2,128)S(1)}, f32[4,128,128]{2,1,0:T(8,128)S(1)}, s32[]{:T(128)}) %tuple.128), condition=%wide.while_cond.clone.1, body=%wide.while_body.clone.1.sunk | while | flops 2 | bytes 131189 | solution.py:115
  1053.0 39.3 %custom-call.42 = f32[4,128,128]{1,2,0:T(8,128)S(1)} custom-call(f32[4,128,128]{2,1,0:T(8,128)S(1)} %get-tuple-element.33), custom_call_target="InvertDiagBlocksLowerTriangular" | custom-call | tf_op jit(solution)/shard_map/triangular_solve/custom-call.3 | solution.py:115
  (266 shorter events, 264.4 us)
Async XLA Ops:
  7.2 48.7 %all-gather.4.cloned.1.call-start = ((), (), s32[]{:S(2)}) async-start(), calls=%async_computation | async-start | bytes 1966080 | tf_op jit(solution)/shard_map/all_gather | solution.py:25
  7.2 10.5 collective-permute-start
  21.5 1.1 copy-start.6
  21.5 1.2 copy-start.8
  23.9 1.0 copy-start.3
  25.7 229.8 %all-gather.6.cloned.1.call-start = ((), (), s32[]{:S(2)}) async-start(), calls=%async_computation.1 | async-start | bytes 2621440 | tf_op jit(solution)/shard_map/all_gather | solution.py:25
  55.9 4.4 collective-permute-start.1
  65.7 1.0 copy-start
  218.2 0.7 copy-start.4
  222.1 378.4 %all-gather.8.cloned.1.call-start = ((), (), s32[]{:S(2)}) async-start(), calls=%async_computation.2 | async-start | bytes 1310720 | tf_op jit(solution)/shard_map/all_gather | solution.py:25
  255.5 4.8 collective-permute-start.2
  265.4 92.1 %collective-permute-start.3 = (f32[1024,1024]{1,0:T(8,128)}, f32[1024,1024]{1,0:T(8,128)}, u32[]{:S(2)}, u32[]{:S(2)}) collective-permute-start(f32[1024,1024]{1,0:T(8,128)} %maximum_select_fusion), channel_id=1, source_target_pairs={{0,8},{8,0},{4,12},{12,4},{16,24},{24,16},{20,28},{28,20},{32,40},... | collective-permute-start | bytes 12582920 | tf_op jit(solution)/shard_map/ppermute | solution.py:21
  360.6 1.0 copy-start.7
  360.6 1.0 copy-start.10
  362.2 15.5 %copy-start.5 = (f32[96,1536]{1,0:T(8,128)}, f32[96,1536]{1,0:T(8,128)S(1)}, u32[]{:S(2)}) copy-start(f32[96,1536]{1,0:T(8,128)S(1)} %bitcast_add_fusion.5) | copy-start | bytes 1769476
  372.9 6.7 collective-permute-start.4
  379.7 35.7 %collective-permute-start.5 = (f32[768,512]{1,0:T(8,128)S(1)}, f32[768,512]{1,0:T(8,128)S(1)}, u32[]{:S(2)}, u32[]{:S(2)}) collective-permute-start(f32[768,512]{1,0:T(8,128)S(1)} %maximum_select_fusion.6), channel_id=1, source_target_pairs={{0,8},{8,0},{4,12},{12,4},{16,24},{24,16},{20,28},{28,20},{32,40},... | collective-permute-start | bytes 4718600 | tf_op jit(solution)/shard_map/ppermute | solution.py:21
  418.8 1.0 copy-start.1
  600.5 4.5 collective-permute-start.6
  606.8 51.6 %copy-start.12 = (s32[16,8]{0,1:T(8,128)S(1)}, s32[16,8]{0,1:T(8,128)}, u32[]{:S(2)}) copy-start(s32[16,8]{0,1:T(8,128)} %param.28) | copy-start | bytes 1540
  606.8 46.9 %collective-permute-start.7 = (f32[512,1024]{1,0:T(8,128)S(1)}, f32[512,1024]{1,0:T(8,128)S(1)}, u32[]{:S(2)}, u32[]{:S(2)}) collective-permute-start(f32[512,1024]{1,0:T(8,128)S(1)} %maximum_select_fusion.5), channel_id=1, source_target_pairs={{0,8},{8,0},{4,12},{12,4},{16,24},{24,16},{20,28},{28,20},{32,40},... | collective-permute-start | bytes 6291464 | tf_op jit(solution)/shard_map/ppermute | solution.py:21
  656.1 182.5 %collective-permute-start.8 = (f32[1024,1024]{1,0:T(8,128)}, f32[1024,1024]{1,0:T(8,128)}, u32[]{:S(2)}, u32[]{:S(2)}) collective-permute-start(f32[1024,1024]{1,0:T(8,128)} %maximum_select_fusion.1), channel_id=1, source_target_pairs={{0,16},{16,0},{4,20},{20,4},{8,24},{24,8},{12,28},{28,12},{32,48},... | collective-permute-start | bytes 12582920 | tf_op jit(solution)/shard_map/ppermute | solution.py:21
  841.6 0.9 copy-start.9
  841.6 1.0 copy-start.11
  853.5 4.9 collective-permute-start.9
  858.4 18.8 %collective-permute-start.10 = (f32[384,512]{1,0:T(8,128)S(1)}, f32[384,512]{1,0:T(8,128)S(1)}, u32[]{:S(2)}, u32[]{:S(2)}) collective-permute-start(f32[384,512]{1,0:T(8,128)S(1)} %maximum_select_fusion.8), channel_id=1, source_target_pairs={{0,8},{8,0},{4,12},{12,4},{16,24},{24,16},{20,28},{28,20},{32,40},... | collective-permute-start | bytes 2359304 | tf_op jit(solution)/shard_map/ppermute | solution.py:21
  877.5 70.5 %collective-permute-start.11 = (f32[768,512]{1,0:T(8,128)S(1)}, f32[768,512]{1,0:T(8,128)S(1)}, u32[]{:S(2)}, u32[]{:S(2)}) collective-permute-start(f32[768,512]{1,0:T(8,128)S(1)} %maximum_select_fusion.7), channel_id=1, source_target_pairs={{0,16},{16,0},{4,20},{20,4},{8,24},{24,8},{12,28},{28,12},{32,48},... | collective-permute-start | bytes 4718600 | tf_op jit(solution)/shard_map/ppermute | solution.py:21
  951.3 1.0 copy-start.2
Sparse Core Ops, SparseCore 0:
  25.8 30.0 all-gather.3
  222.2 33.1 all-gather.5
  574.6 25.8 all-gather.7
where the time goes:
time: 1120 us; the launch traced here: 1110 us
  waiting for transfers between devices  528 us (47%)
  other arithmetic  382 us (34%)
  local copies, waits for them, and re-layouts  74.5 us (7%)
  matrix products  59 us (5%)
  starting transfers between devices  24.1 us (2%)
  between operations  22.8 us (2%)
  blocking collectives  21.5 us (2%)
    ppermute x12, waiting for transfers between devices, from_partner(): return lax.ppermute(block, axis, route)  438 us
    another operation x45, other arithmetic, body(): diag_factor = jnp.linalg.cholesky(pivot_block)  238 us
    another operation x10, other arithmetic, body(): lax.linalg.triangular_solve(diag_factor, lower_block, left_side=False, lo...  123 us
    all_gather x3, waiting for transfers between devices, collect(): gathered = lax.all_gather(pieces, 'front', axis=0, tiled=True)  89.5 us
    another operation x40, local copies, waits for them, and re-layouts, body(): lax.linalg.triangular_solve(diag_factor, lower_block, left_side=False, lo...  34.4 us
    another operation x21, matrix products, body(): lax.linalg.triangular_solve(diag_factor, lower_block, left_side=False, lo...  32.4 us
    ppermute x12, starting transfers between devices, from_partner(): return lax.ppermute(block, axis, route)  24 us
  transfers between devices with their start and end apart: 15, of which 15 were waited for; matrix products, arithmetic and copies ran while one was open for 2% of the time, Pallas kernels for 0%

commit v1 on v0

--- a/solution.py
+++ b/solution.py
@@ -11,6 +11,28 @@
 UT = 8
 
 
+def in_order(parts, dim):
+    lengths = list(parts.shape[1:])
+    lengths[dim] *= parts.shape[0]
+    return jnp.moveaxis(parts, 0, dim).reshape(lengths)
+
+
+def collect_2(array, axis, dim):
+    length = lax.axis_size(axis)
+    pairs = [(i, (i + 1) % length) for i in range(length)]
+    back = [(b, a) for a, b in pairs]
+    lower, upper = ([], [])
+    for step in range(length - 1):
+        if step % 2 == 0:
+            lower.append(lax.ppermute(lower[-1] if lower else array, axis, pairs))
+        else:
+            upper.append(lax.ppermute(upper[-1] if upper else array, axis, back))
+    parts = jnp.stack([*lower[::-1], array, *upper])
+    shift = lax.axis_index(axis) - len(lower)
+    parts = parts[(jnp.arange(length) - shift) % length]
+    return in_order(parts, dim)
+
+
 def from_partner(block, axis, stride):
     count = lax.axis_size(axis)
     route = []
@@ -22,7 +44,7 @@
 
 
 def collect(pieces, depth_count):
-    gathered = lax.all_gather(pieces, "front", axis=0, tiled=True)
+    gathered = collect_2(pieces, "front", 0)
     leaf_place = lax.axis_index("leaf")
     for bit_number in range(depth_count):
         partner = from_partner(gathered, "leaf", bit_number)

time: 1120 us -> 1090 us (0.973)
  blocking collectives: 21.5 us -> 0 us
  between operations: 22.8 us -> 10 us
  starting transfers between devices: 24.1 us -> 36.5 us
  waiting for transfers between devices: 528 us -> 516 us
    all_gather x3 -> x0, waiting for transfers between devices: 89.5 us -> none  [collect(): gathered = lax.all_gather(pieces, 'front', axis=0, tiled=True)]
    ppermute x0 -> x15, waiting for transfers between devices: none -> 72.7 us  [the longest x10 72.7 us: collect_2(): lower.append(lax.ppermute(lower[-1] if lower else array, axis, pairs))]
    all_gather x2 -> x0, blocking collectives: 21.5 us -> none  [collect(): gathered = lax.all_gather(pieces, 'front', axis=0, tiled=True)]
    ppermute x0 -> x15, starting transfers between devices: none -> 14.4 us  [the longest x5 13.3 us: collect_2(): upper.append(lax.ppermute(upper[-1] if upper else array, axis, back))]
  transfers between devices with their start and end apart: 15 -> 27, of which waited for: 15 -> 22; matrix products, arithmetic and copies ran while one was open for 2% -> 2% of each run, Pallas kernels for 0% -> 0%
where the time goes in v1:
time: 1090 us; the launch traced here: 1080 us
  waiting for transfers between devices  516 us (47%)
  other arithmetic  379 us (35%)
  local copies, waits for them, and re-layouts  77.6 us (7%)
  matrix products  57.6 us (5%)
  starting transfers between devices  36.5 us (3%)
    ppermute x12, waiting for transfers between devices, from_partner(): return lax.ppermute(block, axis, route)  443 us
    another operation x45, other arithmetic, body(): diag_factor = jnp.linalg.cholesky(pivot_block)  238 us
    another operation x10, other arithmetic, body(): lax.linalg.triangular_solve(diag_factor, lower_block, left_side=False, lo...  123 us
    ppermute x10, waiting for transfers between devices, collect_2(): lower.append(lax.ppermute(lower[-1] if lower else array, axis, pairs))  72.7 us
    another operation x40, local copies, waits for them, and re-layouts, body(): lax.linalg.triangular_solve(diag_factor, lower_block, left_side=False, lo...  34.4 us
    another operation x21, matrix products, body(): lax.linalg.triangular_solve(diag_factor, lower_block, left_side=False, lo...  32.4 us
    ppermute x12, starting transfers between devices, from_partner(): return lax.ppermute(block, axis, route)  22.2 us
  transfers between devices with their start and end apart: 27, of which 22 were waited for; matrix products, arithmetic and copies ran while one was open for 2% of the time, Pallas kernels for 0%

profile of v1, /device:TPU:1, one launch (start us, length us, event | category | flops | bytes accessed | tf_op | source)
XLA Modules:
  0.0 1076.9 jit_solution(3396033934330308224)
XLA Ops:
  30.1 10.6 collective-permute-done.2
  51.3 11.7 %cholesky.374 = f32[128,128]{1,0:T(8,128)S(1)} custom-call(f32[128,128]{1,0:T(8,128)S(1)} %cholesky.586), custom_call_target="Cholesky" | custom-call | tf_op jit(solution)/shard_map/jit(cholesky)/cholesky | solution.py:136
  75.5 11.7 %cholesky.393 = f32[128,128]{1,0:T(8,128)S(1)} custom-call(f32[128,128]{1,0:T(8,128)S(1)} %cholesky.590), custom_call_target="Cholesky" | custom-call | tf_op jit(solution)/shard_map/jit(cholesky)/cholesky | solution.py:136
  87.3 10.2 custom-call.32
  99.1 11.7 %cholesky.414 = f32[128,128]{1,0:T(8,128)S(1)} custom-call(f32[128,128]{1,0:T(8,128)S(1)} %cholesky.595), custom_call_target="Cholesky" | custom-call | tf_op jit(solution)/shard_map/jit(cholesky)/cholesky | solution.py:136
  110.8 9.8 custom-call.33
  122.1 11.7 %cholesky.431 = f32[128,128]{1,0:T(8,128)S(1)} custom-call(f32[128,128]{1,0:T(8,128)S(1)} %convolution_subtract_fusion.10), custom_call_target="Cholesky" | custom-call | tf_op jit(solution)/shard_map/jit(cholesky)/cholesky | solution.py:136
  140.7 11.7 %while.6 = (s32[]{:T(128)}, f32[512,512]{1,0:T(8,128)}, s32[4,2]{0,1:T(2,128)S(1)}, f32[4,128,128]{2,1,0:T(8,128)S(1)}, s32[]{:T(128)}) while((s32[]{:T(128)}, f32[512,512]{1,0:T(8,128)}, s32[4,2]{0,1:T(2,128)S(1)}, f32[4,128,128]{2,1,0:T(8,128)S(1)}, s32[]{:T(128)}) %tuple.114), condition=%wide.while_cond, body=%wide.while_body.sunk | while | flops 2 | bytes 131189 | solution.py:137
  152.4 39.3 %custom-call.34 = f32[4,128,128]{1,2,0:T(8,128)S(1)} custom-call(f32[4,128,128]{2,1,0:T(8,128)S(1)} %get-tuple-element.31), custom_call_target="InvertDiagBlocksLowerTriangular" | custom-call | tf_op jit(solution)/shard_map/triangular_solve/custom-call.3 | solution.py:137
  208.4 11.7 %collective-permute-done.5 = f32[128,1024]{1,0:T(8,128)S(1)} collective-permute-done((f32[128,1024]{1,0:T(8,128)S(1)}, f32[128,1024]{1,0:T(8,128)S(1)}, u32[]{:S(2)}, u32[]{:S(2)}) %collective-permute-start.5) | collective-permute-done | bytes 524320 | tf_op jit(solution)/shard_map/ppermute | solution.py:27
  220.1 13.4 %collective-permute-done.6 = f32[128,1024]{1,0:T(8,128)S(1)} collective-permute-done((f32[128,1024]{1,0:T(8,128)S(1)}, f32[128,1024]{1,0:T(8,128)S(1)}, u32[]{:S(2)}, u32[]{:S(2)}) %collective-permute-start.6) | collective-permute-done | bytes 524320 | tf_op jit(solution)/shard_map/ppermute | solution.py:27
  251.2 87.8 %collective-permute-done.9 = f32[1024,1024]{1,0:T(8,128)} collective-permute-done((f32[1024,1024]{1,0:T(8,128)}, f32[1024,1024]{1,0:T(8,128)}, u32[]{:S(2)}, u32[]{:S(2)}) %collective-permute-start.9) | collective-permute-done | bytes 4194336 | tf_op jit(solution)/shard_map/ppermute | solution.py:43
  362.7 35.6 %collective-permute-done.14 = f32[768,512]{1,0:T(8,128)S(1)} collective-permute-done((f32[768,512]{1,0:T(8,128)S(1)}, f32[768,512]{1,0:T(8,128)S(1)}, u32[]{:S(2)}, u32[]{:S(2)}) %collective-permute-start.14) | collective-permute-done | bytes 1572896 | tf_op jit(solution)/shard_map/ppermute | solution.py:43
  402.6 11.7 %cholesky.446 = f32[128,128]{1,0:T(8,128)S(1)} custom-call(f32[128,128]{1,0:T(8,128)S(1)} %cholesky.599), custom_call_target="Cholesky" | custom-call | tf_op jit(solution)/shard_map/jit(cholesky)/cholesky | solution.py:136
  426.8 11.7 %cholesky.465 = f32[128,128]{1,0:T(8,128)S(1)} custom-call(f32[128,128]{1,0:T(8,128)S(1)} %cholesky.603), custom_call_target="Cholesky" | custom-call | tf_op jit(solution)/shard_map/jit(cholesky)/cholesky | solution.py:136
  438.5 10.0 custom-call.36
  450.1 11.7 %cholesky.486 = f32[128,128]{1,0:T(8,128)S(1)} custom-call(f32[128,128]{1,0:T(8,128)S(1)} %cholesky.608), custom_call_target="Cholesky" | custom-call | tf_op jit(solution)/shard_map/jit(cholesky)/cholesky | solution.py:136
  461.8 9.8 custom-call.37
  473.1 11.7 %cholesky.503 = f32[128,128]{1,0:T(8,128)S(1)} custom-call(f32[128,128]{1,0:T(8,128)S(1)} %convolution_subtract_fusion.9), custom_call_target="Cholesky" | custom-call | tf_op jit(solution)/shard_map/jit(cholesky)/cholesky | solution.py:136
  491.6 11.8 %while.7 = (s32[]{:T(128)}, f32[512,512]{1,0:T(8,128)}, s32[4,2]{0,1:T(2,128)S(1)}, f32[4,128,128]{2,1,0:T(8,128)S(1)}, s32[]{:T(128)}) while((s32[]{:T(128)}, f32[512,512]{1,0:T(8,128)}, s32[4,2]{0,1:T(2,128)S(1)}, f32[4,128,128]{2,1,0:T(8,128)S(1)}, s32[]{:T(128)}) %tuple.123), condition=%wide.while_cond.clone, body=%wide.while_body.clone.sunk | while | flops 2 | bytes 131189 | solution.py:137
  503.3 39.3 %custom-call.38 = f32[4,128,128]{1,2,0:T(8,128)S(1)} custom-call(f32[4,128,128]{2,1,0:T(8,128)S(1)} %get-tuple-element.32), custom_call_target="InvertDiagBlocksLowerTriangular" | custom-call | tf_op jit(solution)/shard_map/triangular_solve/custom-call.3 | solution.py:137
  578.1 46.8 %collective-permute-done.19 = f32[512,1024]{1,0:T(8,128)S(1)} collective-permute-done((f32[512,1024]{1,0:T(8,128)S(1)}, f32[512,1024]{1,0:T(8,128)S(1)}, u32[]{:S(2)}, u32[]{:S(2)}) %collective-permute-start.19) | collective-permute-done | bytes 2097184 | tf_op jit(solution)/shard_map/ppermute | solution.py:43
  633.0 177.5 %collective-permute-done.20 = f32[1024,1024]{1,0:T(8,128)} collective-permute-done((f32[1024,1024]{1,0:T(8,128)}, f32[1024,1024]{1,0:T(8,128)}, u32[]{:S(2)}, u32[]{:S(2)}) %collective-permute-start.20) | collective-permute-done | bytes 4194336 | tf_op jit(solution)/shard_map/ppermute | solution.py:43
  829.2 18.7 %collective-permute-done.25 = f32[384,512]{1,0:T(8,128)S(1)} collective-permute-done((f32[384,512]{1,0:T(8,128)S(1)}, f32[384,512]{1,0:T(8,128)S(1)}, u32[]{:S(2)}, u32[]{:S(2)}) %collective-permute-start.25) | collective-permute-done | bytes 786464 | tf_op jit(solution)/shard_map/ppermute | solution.py:43
  855.8 63.2 %collective-permute-done.26 = f32[768,512]{1,0:T(8,128)S(1)} collective-permute-done((f32[768,512]{1,0:T(8,128)S(1)}, f32[768,512]{1,0:T(8,128)S(1)}, u32[]{:S(2)}, u32[]{:S(2)}) %collective-permute-start.26) | collective-permute-done | bytes 1572896 | tf_op jit(solution)/shard_map/ppermute | solution.py:43
  923.3 11.7 %cholesky.518 = f32[128,128]{1,0:T(8,128)S(1)} custom-call(f32[128,128]{1,0:T(8,128)S(1)} %cholesky.612), custom_call_target="Cholesky" | custom-call | tf_op jit(solution)/shard_map/jit(cholesky)/cholesky | solution.py:136
  947.5 11.7 %cholesky.537 = f32[128,128]{1,0:T(8,128)S(1)} custom-call(f32[128,128]{1,0:T(8,128)S(1)} %cholesky.616), custom_call_target="Cholesky" | custom-call | tf_op jit(solution)/shard_map/jit(cholesky)/cholesky | solution.py:136
  959.3 10.0 custom-call.40
  970.8 11.7 %cholesky.558 = f32[128,128]{1,0:T(8,128)S(1)} custom-call(f32[128,128]{1,0:T(8,128)S(1)} %cholesky.621), custom_call_target="Cholesky" | custom-call | tf_op jit(solution)/shard_map/jit(cholesky)/cholesky | solution.py:136
  993.8 12.0 %cholesky.575 = f32[128,128]{1,0:T(8,128)S(1)} custom-call(f32[128,128]{1,0:T(8,128)S(1)} %convolution_subtract_fusion.8), custom_call_target="Cholesky" | custom-call | tf_op jit(solution)/shard_map/jit(cholesky)/cholesky | solution.py:136
  1012.7 11.5 %while.8 = (s32[]{:T(128)}, f32[512,512]{1,0:T(8,128)}, s32[4,2]{0,1:T(2,128)S(1)}, f32[4,128,128]{2,1,0:T(8,128)S(1)}, s32[]{:T(128)}) while((s32[]{:T(128)}, f32[512,512]{1,0:T(8,128)}, s32[4,2]{0,1:T(2,128)S(1)}, f32[4,128,128]{2,1,0:T(8,128)S(1)}, s32[]{:T(128)}) %tuple.124), condition=%wide.while_cond.clone.1, body=%wide.while_body.clone.1.sunk | while | flops 2 | bytes 131189 | solution.py:137
  1024.1 39.3 %custom-call.42 = f32[4,128,128]{1,2,0:T(8,128)S(1)} custom-call(f32[4,128,128]{2,1,0:T(8,128)S(1)} %get-tuple-element.33), custom_call_target="InvertDiagBlocksLowerTriangular" | custom-call | tf_op jit(solution)/shard_map/triangular_solve/custom-call.3 | solution.py:137
  (297 shorter events, 292.5 us)
Async XLA Ops:
  0.6 10.5 collective-permute-start
  14.9 1.1 copy-start.6
  14.9 1.2 copy-start.8
  18.4 11.6 %collective-permute-start.1 = (f32[192,512]{1,0:T(8,128)S(1)}, f32[192,512]{1,0:T(8,128)S(1)}, u32[]{:S(2)}, u32[]{:S(2)}) collective-permute-start(f32[192,512]{1,0:T(8,128)S(1)} %get-tuple-element.127), channel_id=1, source_target_pairs={{0,1},{1,2},{2,3},{3,0},{4,5},{5,6},{6,7},{7,4},{8,9},{9,10},{10,1... | collective-permute-start | bytes 1179656 | tf_op jit(solution)/shard_map/ppermute | solution.py:27
  18.5 11.6 %collective-permute-start.3 = (f32[192,512]{1,0:T(8,128)S(1)}, f32[192,512]{1,0:T(8,128)S(1)}, u32[]{:S(2)}, u32[]{:S(2)}) collective-permute-start(f32[192,512]{1,0:T(8,128)S(1)} %get-tuple-element.127), channel_id=1, source_target_pairs={{1,0},{2,1},{3,2},{0,3},{5,4},{6,5},{7,6},{4,7},{9,8},{10,9},{11,1... | collective-permute-start | bytes 1179656 | tf_op jit(solution)/shard_map/ppermute | solution.py:29
  30.0 10.6 collective-permute-start.2
  41.4 5.5 collective-permute-start.4
  202.9 30.5 %copy-start.4 = (f32[128,512]{0,1:T(8,128)}, f32[128,512]{0,1:T(8,128)S(1)}, u32[]{:S(2)}) copy-start(f32[128,512]{0,1:T(8,128)S(1)} %constant_dynamic-slice_fusion.10) | copy-start | bytes 786436
  205.4 14.6 %collective-permute-start.5 = (f32[128,1024]{1,0:T(8,128)S(1)}, f32[128,1024]{1,0:T(8,128)S(1)}, u32[]{:S(2)}, u32[]{:S(2)}) collective-permute-start(f32[128,1024]{1,0:T(8,128)S(1)} %convolution_subtract_fusion), channel_id=1, source_target_pairs={{0,1},{1,2},{2,3},{3,0},{4,5},{5,6},{6,7},{7,4},{8,9},{9,10},{10,1... | collective-permute-start | bytes 1572872 | tf_op jit(solution)/shard_map/ppermute | solution.py:27
  205.7 14.3 %collective-permute-start.7 = (f32[128,1024]{1,0:T(8,128)S(1)}, f32[128,1024]{1,0:T(8,128)S(1)}, u32[]{:S(2)}, u32[]{:S(2)}) collective-permute-start(f32[128,1024]{1,0:T(8,128)S(1)} %convolution_subtract_fusion), channel_id=1, source_target_pairs={{1,0},{2,1},{3,2},{0,3},{5,4},{6,5},{7,6},{4,7},{9,8},{10,9},{11,1... | collective-permute-start | bytes 1572872 | tf_op jit(solution)/shard_map/ppermute | solution.py:29
  220.0 13.4 %collective-permute-start.6 = (f32[128,1024]{1,0:T(8,128)S(1)}, f32[128,1024]{1,0:T(8,128)S(1)}, u32[]{:S(2)}, u32[]{:S(2)}) collective-permute-start(f32[128,1024]{1,0:T(8,128)S(1)} %collective-permute-done.5), channel_id=1, source_target_pairs={{0,1},{1,2},{2,3},{3,0},{4,5},{5,6},{6,7},{7,4},{8,9},{9,10},{10,1... | collective-permute-start | bytes 1572872 | tf_op jit(solution)/shard_map/ppermute | solution.py:27
  235.7 6.1 collective-permute-start.8
  246.9 92.1 %collective-permute-start.9 = (f32[1024,1024]{1,0:T(8,128)}, f32[1024,1024]{1,0:T(8,128)}, u32[]{:S(2)}, u32[]{:S(2)}) collective-permute-start(f32[1024,1024]{1,0:T(8,128)} %maximum_select_fusion), channel_id=1, source_target_pairs={{0,8},{8,0},{4,12},{12,4},{16,24},{24,16},{20,28},{28,20},{32,40},... | collective-permute-start | bytes 12582920 | tf_op jit(solution)/shard_map/ppermute | solution.py:43
  343.7 12.3 %copy-start.5 = (f32[96,1536]{1,0:T(8,128)}, f32[96,1536]{1,0:T(8,128)S(1)}, u32[]{:S(2)}) copy-start(f32[96,1536]{1,0:T(8,128)S(1)} %bitcast_add_fusion.5) | copy-start | bytes 1769476
  343.8 6.5 collective-permute-start.10
  343.8 6.4 collective-permute-start.12
  350.2 5.7 collective-permute-start.11
  356.6 5.3 collective-permute-start.13
  362.1 36.1 %collective-permute-start.14 = (f32[768,512]{1,0:T(8,128)S(1)}, f32[768,512]{1,0:T(8,128)S(1)}, u32[]{:S(2)}, u32[]{:S(2)}) collective-permute-start(f32[768,512]{1,0:T(8,128)S(1)} %maximum_select_fusion.6), channel_id=1, source_target_pairs={{0,8},{8,0},{4,12},{12,4},{16,24},{24,16},{20,28},{28,20},{32,40},... | collective-permute-start | bytes 4718600 | tf_op jit(solution)/shard_map/ppermute | solution.py:43
  556.3 8.3 collective-permute-start.15
  556.8 7.8 collective-permute-start.17
  564.6 6.9 collective-permute-start.16
  572.3 5.4 collective-permute-start.18
  577.9 51.0 %copy-start.12 = (s32[16,8]{0,1:T(8,128)S(1)}, s32[16,8]{0,1:T(8,128)}, u32[]{:S(2)}) copy-start(s32[16,8]{0,1:T(8,128)} %param.28) | copy-start | bytes 1540
  577.9 46.9 %collective-permute-start.19 = (f32[512,1024]{1,0:T(8,128)S(1)}, f32[512,1024]{1,0:T(8,128)S(1)}, u32[]{:S(2)}, u32[]{:S(2)}) collective-permute-start(f32[512,1024]{1,0:T(8,128)S(1)} %maximum_select_fusion.5), channel_id=1, source_target_pairs={{0,8},{8,0},{4,12},{12,4},{16,24},{24,16},{20,28},{28,20},{32,40},... | collective-permute-start | bytes 6291464 | tf_op jit(solution)/shard_map/ppermute | solution.py:43
  627.2 183.2 %collective-permute-start.20 = (f32[1024,1024]{1,0:T(8,128)}, f32[1024,1024]{1,0:T(8,128)}, u32[]{:S(2)}, u32[]{:S(2)}) collective-permute-start(f32[1024,1024]{1,0:T(8,128)} %maximum_select_fusion.1), channel_id=1, source_target_pairs={{0,16},{16,0},{4,20},{20,4},{8,24},{24,8},{12,28},{28,12},{32,48},... | collective-permute-start | bytes 12582920 | tf_op jit(solution)/shard_map/ppermute | solution.py:43
  814.4 4.8 collective-permute-start.21
  814.5 4.7 collective-permute-start.23
  819.1 4.7 collective-permute-start.22
  824.4 4.7 collective-permute-start.24
  829.1 18.8 %collective-permute-start.25 = (f32[384,512]{1,0:T(8,128)S(1)}, f32[384,512]{1,0:T(8,128)S(1)}, u32[]{:S(2)}, u32[]{:S(2)}) collective-permute-start(f32[384,512]{1,0:T(8,128)S(1)} %maximum_select_fusion.8), channel_id=1, source_target_pairs={{0,8},{8,0},{4,12},{12,4},{16,24},{24,16},{20,28},{28,20},{32,40},... | collective-permute-start | bytes 2359304 | tf_op jit(solution)/shard_map/ppermute | solution.py:43
  848.2 70.8 %collective-permute-start.26 = (f32[768,512]{1,0:T(8,128)S(1)}, f32[768,512]{1,0:T(8,128)S(1)}, u32[]{:S(2)}, u32[]{:S(2)}) collective-permute-start(f32[768,512]{1,0:T(8,128)S(1)} %maximum_select_fusion.7), channel_id=1, source_target_pairs={{0,16},{16,0},{4,20},{20,4},{8,24},{24,8},{12,28},{28,12},{32,48},... | collective-permute-start | bytes 4718600 | tf_op jit(solution)/shard_map/ppermute | solution.py:43
  (8 other events, 8.0 us)
